TPU v7x, 32 devices: a whole 2x2x4 slice. The times are simulated.
32 devices in a mesh: groups: 2 (over y), pool: 4 (over z), sub: 2 (over x), chip: 2 (over core).
Axes of the slice: x: 2, y: 2, z: 4, core: 2. Of those that a mesh axis runs over, the one named last changes fastest.
Arguments:
- hidden: bfloat16 [1024, 4096], P(('groups', 'pool', 'sub', 'chip')), parts along dimension 0, may hold values from -6 to 6
- query_weight_matrix: bfloat16 [4096, 4096], P(None, 'pool'), may hold values from -0.09375 to 0.09375
- adapter_down_weight: bfloat16 [64, 64, 4096], P('pool', None, ('sub', 'chip')), may hold values from -0.09375 to 0.09375
- adapter_up_weight: bfloat16 [64, 64, 4096], P('pool', None, ('sub', 'chip')), may hold values from -0.75 to 0.75
- adapter_index_rows: int32 [1024], P(('groups', 'pool', 'sub', 'chip')), parts along dimension 0, may hold values from 0 to 63, as said below
Outputs:
- query: bfloat16 [1024, 4096], P(('groups', 'pool', 'sub', 'chip')), parts along dimension 0
There are 2 independent parts, one for each index of `groups`. A program takes and returns all parts, laid end to end along the dimension named above; an argument that names none is the same for every part. Nothing has to cross between parts.
Inputs may be any that keep to these rules, and one draw needn't show every extreme that they name: A row's owner is adapter_index_rows // 16. In each aligned block of 32 rows (the rows of one device) at most 12 rows have one owner, and in every block some owner has exactly 12 rows.
All inputs are finite; a program needn't handle non-finite values.
Results may differ from a plain program's by a relative error of at most 0.0052.
Values may be sent and summed in bfloat16 or wider, within the bound.
A program may use at most 64 MiB of HBM per device.

v0:
```python
import jax
import jax.numpy as jnp
from jax import lax
from jax.sharding import PartitionSpec as P

ADAPTER_SCALE = 0.5


def owner_rank(owner, count):
    table = (owner[:, None] == jnp.arange(count, dtype=jnp.int32)[None, :]).astype(jnp.int32)
    running = jnp.cumsum(table, axis=0) - table
    return jnp.sum(running * table, axis=1)


def reduced_rank_term(incoming_rows, nearby_adapters, adapter_down_weight, adapter_up_weight):
    adapter_stack, rank_extent, portion_width = adapter_down_weight.shape
    flattened_down = adapter_down_weight.reshape(adapter_stack * rank_extent, portion_width)
    project = lax.dot_general(
        incoming_rows, flattened_down, (((1,), (1,)), ((), ())), preferred_element_type=jnp.float32
    )
    select = nearby_adapters[:, None] == jnp.arange(adapter_stack, dtype=jnp.int32)[None, :]
    partial_low = jnp.sum(
        project.reshape(-1, adapter_stack, rank_extent) * select[:, :, None].astype(jnp.float32),
        axis=1,
    )
    projected_down = lax.psum(partial_low, ("sub", "chip")).astype(jnp.bfloat16)
    spread = (select[:, :, None].astype(jnp.bfloat16) * projected_down[:, None, :]).reshape(
        -1, adapter_stack * rank_extent
    )
    flattened_up = adapter_up_weight.reshape(adapter_stack * rank_extent, portion_width)
    update_term = jnp.dot(spread, flattened_up, preferred_element_type=jnp.float32)
    return (ADAPTER_SCALE * update_term).astype(jnp.bfloat16)


def local(hidden, query_weight_matrix, adapter_down_weight, adapter_up_weight, adapter_index_rows):
    pools = lax.axis_size("pool")
    shards = lax.axis_size(("sub", "chip"))
    shard_index = lax.axis_index(("sub", "chip"))
    row_count, width = hidden.shape
    adapter_stack = adapter_down_weight.shape[0]
    portion_width = adapter_down_weight.shape[2]
    capacity = 2 + row_count // (pools - 1)
    nothing = jnp.zeros((), jnp.bfloat16)
    query_cols = jnp.dot(
        lax.all_gather(hidden, "pool", axis=0, tiled=True),
        query_weight_matrix,
        preferred_element_type=jnp.float32,
    ).astype(jnp.bfloat16)
    block_rows, block_adapters = (
        lax.all_gather(hidden, ("sub", "chip"), axis=0, tiled=True),
        lax.all_gather(adapter_index_rows, ("sub", "chip"), axis=0, tiled=True),
    )
    block_size = shards * row_count
    per_owner = shards * capacity
    combined_output = pools * per_owner
    owner = block_adapters // adapter_stack
    slot = owner * per_owner + owner_rank(owner, pools)
    slot_row = (
        jnp.full((combined_output,), -1, jnp.int32)
        .at[slot]
        .set(jnp.arange(block_size, dtype=jnp.int32))
    )
    filled = slot_row >= 0
    safe_row = jnp.maximum(slot_row, 0)
    my_slice = lax.dynamic_slice_in_dim(block_rows, shard_index * portion_width, portion_width, 1)
    send_rows = jnp.where(filled[:, None], jnp.take(my_slice, safe_row, axis=0), nothing)
    send_adapters = jnp.where(filled, jnp.take(block_adapters % adapter_stack, safe_row), 0)
    received_rows, received_adapters = (
        lax.all_to_all(
            send_rows.reshape(pools, per_owner, portion_width),
            "pool",
            split_axis=0,
            concat_axis=0,
            tiled=True,
        ),
        lax.all_to_all(
            send_adapters.reshape(pools, per_owner), "pool", split_axis=0, concat_axis=0, tiled=True
        ),
    )
    update_term = reduced_rank_term(
        received_rows.reshape(combined_output, portion_width),
        received_adapters.reshape(combined_output),
        adapter_down_weight,
        adapter_up_weight,
    )
    returned = lax.all_to_all(
        update_term.reshape(pools, per_owner, portion_width),
        "pool",
        split_axis=0,
        concat_axis=0,
        tiled=True,
    )
    delta_block = jnp.take(returned.reshape(combined_output, portion_width), slot, axis=0)
    delta_rows = lax.all_to_all(
        delta_block, ("sub", "chip"), split_axis=0, concat_axis=1, tiled=True
    )
    query = lax.all_to_all(query_cols, "pool", split_axis=0, concat_axis=1, tiled=True)
    return (query.astype(jnp.float32) + delta_rows.astype(jnp.float32)).astype(jnp.bfloat16)


def solution(mesh):
    in_specs = (
        P(("groups", "pool", "sub", "chip"), None),
        P(None, "pool"),
        P("pool", None, ("sub", "chip")),
        P("pool", None, ("sub", "chip")),
        P(("groups", "pool", "sub", "chip")),
    )
    out_specs = P(("groups", "pool", "sub", "chip"), None)
    return jax.shard_map(local, mesh=mesh, in_specs=in_specs, out_specs=out_specs, check_vma=False)
```

profile of v0, /device:TPU:0, one launch (start us, length us, event | category | flops | bytes accessed | tf_op | source)
XLA Modules:
  0.0 115.8 jit_solution(494919803565934389)
XLA Ops:
  6.5 0.7 all-gather.5.cloned.1.call-update
  7.3 1.2 %dynamic-slice = u32[1]{0:T(128)} dynamic-slice(u32[32]{0:T(128)} %constant.102, u32[]{:T(128)S(6)} %add.48), dynamic_slice_sizes={1} | dynamic-slice | bytes 12
  9.2 0.9 dynamic-update-slice
  10.0 6.3 %all-reduce = s32[128]{0:T(128)S(1)} all-reduce(s32[128]{0:T(128)S(1)} %dynamic-update-slice), channel_id=1, replica_groups=mesh['groups'=2,'pool'=4,'sub'=2,'chip'=2] {'sub','chip'}, use_global_device_ids=true, to_apply=%add | all-reduce | flops 128 | bytes 1024
  16.5 0.2 reduce_window_sum.11
  16.7 0.2 select_reduce_fusion
  16.9 1.0 scatter_custom_fusion
  17.9 1.6 %gather_fusion = s32[192]{0:T(256)S(1)} fusion(s32[128]{0:T(128)S(1)} %get-tuple-element.12, s32[1024]{0:T(1024)S(1)} %pad_clamp_fusion.1), kind=kCustom, calls=%fused_computation | custom fusion | bytes 2304 | tf_op jit(solution)/shard_map/jit(_take)/gather | solution.py:67
  19.4 0.7 all_to_all.32
  20.1 4.9 %all-to-all-start.1 = ((s32[4,1,48]{2,1,0:T(1,128)}), s32[4,1,48]{2,1,0:T(1,128)S(1)}, u32[]{:S(2)}, u32[]{:S(2)}) async-start(s32[4,1,48]{2,1,0:T(1,128)} %all_to_all.32), calls=%async_computation.1 | async-start | bytes 4096 | tf_op jit(solution)/shard_map/all_to_all | solution.py:76
  25.0 0.7 all-gather.3.cloned.1.call-update
  25.7 0.1 broadcast_in_dim.67
  25.9 2.5 %all-gather.5.cloned.1.call-done = bf16[128,4096]{1,0:T(8,128)(2,1)} async-done(((bf16[32,4096]{1,0:T(8,128)(2,1)}), bf16[128,4096]{1,0:T(8,128)(2,1)}) %all-gather.5.cloned.1.call-update) | async-done | bytes 1048592 | tf_op jit(solution)/shard_map/all_gather | solution.py:50
  28.4 1.0 constant_dynamic-slice_fusion
  29.3 1.0 gather_fusion.1
  30.4 0.9 select_select_fusion
  31.2 4.6 %all-to-all-start.2 = ((bf16[4,48,1024]{2,1,0:T(8,128)(2,1)}), bf16[4,48,1024]{2,1,0:T(8,128)(2,1)S(1)}, u32[]{:S(2)}, u32[]{:S(2)}) async-start(bf16[4,48,1024]{2,1,0:T(8,128)(2,1)} %select_select_fusion), calls=%async_computation.2 | async-start | bytes 786432 | tf_op jit(solution)/shard_map/all_to_all | solution.py:69
  35.8 0.5 broadcast.96
  36.3 0.7 reduce.3
  37.1 20.6 %all-to-all-done.2 = bf16[4,48,1024]{2,1,0:T(8,128)(2,1)S(1)} async-done(((bf16[4,48,1024]{2,1,0:T(8,128)(2,1)}), bf16[4,48,1024]{2,1,0:T(8,128)(2,1)S(1)}, u32[]{:S(2)}, u32[]{:S(2)}) %all-to-all-start.2) | async-done | bytes 393248 | tf_op jit(solution)/shard_map/all_to_all | solution.py:69
  57.7 2.3 %fusion.2 = f32[192,64]{0,1:T(8,128)S(1)} fusion(bf16[192,1024,1]{1,0,2:T(8,128)(2,1)S(1)} %bitcast.27, bf16[16,64,1024]{2,1,0:T(8,128)(2,1)} %param.7, f32[192,16]{0,1:T(8,128)S(1)} %get-tuple-element.11), kind=kOutput, calls=%fused_computation.8 | convolution fusion | flops 403034112 | bytes 2551808 | tf_op jit(solution)/shard_map/dot_general | solution.py:18
  60.1 11.1 %psum.7 = bf16[192,64]{0,1:T(8,128)(2,1)S(1)} all-reduce(f32[192,64]{0,1:T(8,128)S(1)} %fusion.2), channel_id=1, replica_groups=mesh['groups'=2,'pool'=4,'sub'=2,'chip'=2] {'sub','chip'}, use_global_device_ids=true, to_apply=%region_4.5 | all-reduce | flops 12288 | bytes 73728 | tf_op jit(solution)/shard_map/psum | solution.py:26
  71.2 1.4 %fusion.1 = bf16[192,1024]{1,0:T(8,128)(2,1)} fusion(bf16[16,64,1024]{2,1,0:T(8,128)(2,1)S(1)} %copy-done, bf16[192,64]{0,1:T(8,128)(2,1)S(1)} %psum.7, bf16[192,16]{0,1:T(8,128)(2,1)S(1)} %get-tuple-element.10), kind=kOutput, calls=%fused_computation.7 | convolution fusion | flops 403243008 | bytes 2521088 | tf_op jit(solution)/shard_map/dot_general | solution.py:31
  72.5 3.5 %all-to-all-start.3 = ((bf16[4,48,1024]{2,1,0:T(8,128)(2,1)}), bf16[4,48,1024]{2,1,0:T(8,128)(2,1)S(1)}, u32[]{:S(2)}, u32[]{:S(2)}) async-start(bf16[4,48,1024]{2,1,0:T(8,128)(2,1)} %bitcast.6), calls=%async_computation.3 | async-start | bytes 786432 | tf_op jit(solution)/shard_map/all_to_all | solution.py:86
  76.0 5.7 %convolution_convert_fusion = bf16[128,1024]{1,0:T(8,128)(2,1)} fusion(bf16[128,4096]{1,0:T(8,128)(2,1)} %all-gather.3.cloned.1.call-done, bf16[4096,1024]{1,0:T(8,128)(2,1)} %param.6), kind=kOutput, calls=%fused_computation.9 | convolution fusion | flops 1073872896 | bytes 9699328 | tf_op jit(solution)/shard_map/dot_general | solution.py:44
  81.7 5.7 %all-to-all-done.3 = bf16[4,48,1024]{2,1,0:T(8,128)(2,1)S(1)} async-done(((bf16[4,48,1024]{2,1,0:T(8,128)(2,1)}), bf16[4,48,1024]{2,1,0:T(8,128)(2,1)S(1)}, u32[]{:S(2)}, u32[]{:S(2)}) %all-to-all-start.3) | async-done | bytes 393248 | tf_op jit(solution)/shard_map/all_to_all | solution.py:86
  87.4 3.4 %all-to-all-start = ((bf16[4,32,1024]{2,1,0:T(8,128)(2,1)}), bf16[4,32,1024]{2,1,0:T(8,128)(2,1)S(1)}, u32[]{:S(2)}, u32[]{:S(2)}) async-start(bf16[4,32,1024]{2,1,0:T(8,128)(2,1)} %bitcast), calls=%async_computation | async-start | bytes 524288 | tf_op jit(solution)/shard_map/all_to_all | solution.py:97
  90.9 0.9 gather_fusion.2
  91.7 0.1 broadcast_select_fusion
  91.8 5.7 %all-to-all-done = bf16[4,32,1024]{2,1,0:T(8,128)(2,1)S(1)} async-done(((bf16[4,32,1024]{2,1,0:T(8,128)(2,1)}), bf16[4,32,1024]{2,1,0:T(8,128)(2,1)S(1)}, u32[]{:S(2)}, u32[]{:S(2)}) %all-to-all-start) | async-done | bytes 262176 | tf_op jit(solution)/shard_map/all_to_all | solution.py:97
  97.5 10.6 %all_to_all.42 = bf16[4,32,1024]{2,1,0:T(8,128)(2,1)S(1)} all-to-all(bf16[4,32,1024]{2,1,0:T(8,128)(2,1)S(1)} %broadcast_select_fusion), channel_id=1, replica_groups=mesh['groups'=2,'pool'=4,'sub'=2,'chip'=2] {'sub','chip'}, dimensions={0} | all-to-all | bytes 524288 | tf_op jit(solution)/shard_map/all_to_all | solution.py:94
  108.2 0.7 copy.11
  (20 shorter events, 0.5 us)
Async XLA Ops:
  6.5 64.6 %copy-start = (bf16[16,64,1024]{2,1,0:T(8,128)(2,1)S(1)}, bf16[16,64,1024]{2,1,0:T(8,128)(2,1)}, u32[]{:S(2)}) copy-start(bf16[16,64,1024]{2,1,0:T(8,128)(2,1)} %param.8) | copy-start | bytes 6291460
  6.5 21.8 %all-gather.5.cloned.1.call-start = ((), (), s32[]{:S(2)}) async-start(), calls=%async_computation.6 | async-start | bytes 1310720 | tf_op jit(solution)/shard_map/all_gather | solution.py:50
  20.1 11.1 %all-to-all-start.1 = ((s32[4,1,48]{2,1,0:T(1,128)}), s32[4,1,48]{2,1,0:T(1,128)S(1)}, u32[]{:S(2)}, u32[]{:S(2)}) async-start(s32[4,1,48]{2,1,0:T(1,128)} %all_to_all.32), calls=%async_computation.1 | async-start | bytes 4096 | tf_op jit(solution)/shard_map/all_to_all | solution.py:76
  25.0 51.0 %all-gather.3.cloned.1.call-start = ((), (), s32[]{:S(2)}) async-start(), calls=%async_computation.5 | async-start | bytes 1310720 | tf_op jit(solution)/shard_map/all_gather | solution.py:45
  31.2 26.5 %all-to-all-start.2 = ((bf16[4,48,1024]{2,1,0:T(8,128)(2,1)}), bf16[4,48,1024]{2,1,0:T(8,128)(2,1)S(1)}, u32[]{:S(2)}, u32[]{:S(2)}) async-start(bf16[4,48,1024]{2,1,0:T(8,128)(2,1)} %select_select_fusion), calls=%async_computation.2 | async-start | bytes 786432 | tf_op jit(solution)/shard_map/all_to_all | solution.py:69
  72.5 14.8 %all-to-all-start.3 = ((bf16[4,48,1024]{2,1,0:T(8,128)(2,1)}), bf16[4,48,1024]{2,1,0:T(8,128)(2,1)S(1)}, u32[]{:S(2)}, u32[]{:S(2)}) async-start(bf16[4,48,1024]{2,1,0:T(8,128)(2,1)} %bitcast.6), calls=%async_computation.3 | async-start | bytes 786432 | tf_op jit(solution)/shard_map/all_to_all | solution.py:86
  87.4 10.2 %all-to-all-start = ((bf16[4,32,1024]{2,1,0:T(8,128)(2,1)}), bf16[4,32,1024]{2,1,0:T(8,128)(2,1)S(1)}, u32[]{:S(2)}, u32[]{:S(2)}) async-start(bf16[4,32,1024]{2,1,0:T(8,128)(2,1)} %bitcast), calls=%async_computation | async-start | bytes 524288 | tf_op jit(solution)/shard_map/all_to_all | solution.py:97
Sparse Core Ops, SparseCore 0:
  8.9 19.4 all-gather.4
  29.9 35.1 all-gather.2
where the time goes:
time: 116 us
  waiting for transfers between devices  35.9 us (31%)
  blocking collectives  28.1 us (24%)
  starting transfers between devices  16.3 us (14%)
  between operations  14.2 us (12%)
  local copies, waits for them, and re-layouts  9.72 us (8%)
  matrix products  9.37 us (8%)
  other arithmetic  2.18 us (2%)
    all_to_all x1, waiting for transfers between devices, local(): lax.all_to_all(send_rows.reshape(pools, per_owner, portion_width), 'pool'...  20.6 us
    psum x1, blocking collectives, reduced_rank_term(): projected_down = lax.psum(partial_low, ('sub', 'chip')).astype(jnp.bfloat16)  11.1 us
    all_to_all x1, blocking collectives, local(): lax.all_to_all(delta_block, ('sub', 'chip'), split_axis=0, concat_axis=1,...  10.6 us
    unnamed x1, blocking collectives  6.35 us
    all_to_all x1, waiting for transfers between devices, local(): lax.all_to_all(query_cols, 'pool', split_axis=0, concat_axis=1, tiled=True)  5.69 us
    dot_general x1, matrix products, local(): jnp.dot(lax.all_gather(hidden, 'pool', axis=0, tiled=True), query_weight_...  5.68 us
    all_to_all x1, waiting for transfers between devices, local(): lax.all_to_all(update_term.reshape(pools, per_owner, portion_width), 'poo...  5.67 us
    all_to_all x1, starting transfers between devices, local(): lax.all_to_all(send_adapters.reshape(pools, per_owner), 'pool', split_axi...  4.87 us
  transfers between devices with their start and end apart: 6, of which 4 were waited for; matrix products, arithmetic and copies ran while one was open for 17% of the time, Pallas kernels for 0%

commit v1 on v0

--- a/solution.py
+++ b/solution.py
@@ -23,7 +23,9 @@
         project.reshape(-1, adapter_stack, rank_extent) * select[:, :, None].astype(jnp.float32),
         axis=1,
     )
-    projected_down = lax.psum(partial_low, ("sub", "chip")).astype(jnp.bfloat16)
+    projected_down = jnp.sum(lax.all_gather(partial_low, ("sub", "chip")), axis=0).astype(
+        jnp.bfloat16
+    )
     spread = (select[:, :, None].astype(jnp.bfloat16) * projected_down[:, None, :]).reshape(
         -1, adapter_stack * rank_extent
     )

time: 116 us -> 112 us (0.966)
  blocking collectives: 28.1 us -> 20.5 us
  waiting for transfers between devices: 35.9 us -> 39.1 us
    psum x1 -> x0, blocking collectives: 11.1 us -> none  [reduced_rank_term(): projected_down = lax.psum(partial_low, ('sub', 'chip')).astype(jnp.bfloat16)]
    all_gather x0 -> x1, blocking collectives: none -> 5.79 us  [reduced_rank_term(): lax.all_gather(partial_low, ('sub', 'chip'))]
    all_to_all x1, blocking collectives: 10.6 us -> 8.41 us  [local(): lax.all_to_all(delta_block, ('sub', 'chip'), split_axis=0, concat_axis=1,...]
    all_to_all x1, waiting for transfers between devices: 5.69 us -> 7.81 us  [local(): lax.all_to_all(query_cols, 'pool', split_axis=0, concat_axis=1, tiled=True)]
  transfers between devices with their start and end apart: 6 -> 6, of which waited for: 4 -> 4; matrix products, arithmetic and copies ran while one was open for 17% -> 18% of each run, Pallas kernels for 0% -> 0%
where the time goes in v1:
time: 112 us; the launch traced here: 111 us
  waiting for transfers between devices  39.1 us (35%)
  blocking collectives  20.5 us (18%)
  starting transfers between devices  16.3 us (15%)
  between operations  14.2 us (13%)
  local copies, waits for them, and re-layouts  9.72 us (9%)
  matrix products  9.37 us (8%)
  other arithmetic  2.2 us (2%)
    all_to_all x1, waiting for transfers between devices, local(): lax.all_to_all(send_rows.reshape(pools, per_owner, portion_width), 'pool'...  20.6 us
    all_to_all x1, blocking collectives, local(): lax.all_to_all(delta_block, ('sub', 'chip'), split_axis=0, concat_axis=1,...  8.41 us
    all_to_all x1, waiting for transfers between devices, local(): lax.all_to_all(query_cols, 'pool', split_axis=0, concat_axis=1, tiled=True)  7.81 us
    all_to_all x1, waiting for transfers between devices, local(): lax.all_to_all(update_term.reshape(pools, per_owner, portion_width), 'poo...  6.73 us
    unnamed x1, blocking collectives  6.35 us
    all_gather x1, blocking collectives, reduced_rank_term(): lax.all_gather(partial_low, ('sub', 'chip'))  5.79 us
    dot_general x1, matrix products, local(): jnp.dot(lax.all_gather(hidden, 'pool', axis=0, tiled=True), query_weight_...  5.68 us
    all_to_all x1, starting transfers between devices, local(): lax.all_to_all(send_adapters.reshape(pools, per_owner), 'pool', split_axi...  4.87 us
  transfers between devices with their start and end apart: 6, of which 4 were waited for; matrix products, arithmetic and copies ran while one was open for 18% of the time, Pallas kernels for 0%

profile of v1, /device:TPU:0, one launch (start us, length us, event | category | flops | bytes accessed | tf_op | source)
XLA Modules:
  0.0 111.5 jit_solution(9068175689661893076)
XLA Ops:
  6.5 0.7 all-gather.7.cloned.1.call-update
  7.3 1.2 %dynamic-slice = u32[1]{0:T(128)} dynamic-slice(u32[32]{0:T(128)} %constant.102, u32[]{:T(128)S(6)} %add.46), dynamic_slice_sizes={1} | dynamic-slice | bytes 12
  9.2 0.9 dynamic-update-slice
  10.0 6.3 %all-reduce = s32[128]{0:T(128)S(1)} all-reduce(s32[128]{0:T(128)S(1)} %dynamic-update-slice), channel_id=1, replica_groups=mesh['groups'=2,'pool'=4,'sub'=2,'chip'=2] {'sub','chip'}, use_global_device_ids=true, to_apply=%add | all-reduce | flops 128 | bytes 1024
  16.5 0.2 reduce_window_sum.11
  16.7 0.2 select_reduce_fusion
  16.9 1.0 scatter_custom_fusion
  17.9 1.6 %gather_fusion = s32[192]{0:T(256)S(1)} fusion(s32[128]{0:T(128)S(1)} %get-tuple-element.12, s32[1024]{0:T(1024)S(1)} %pad_clamp_fusion.1), kind=kCustom, calls=%fused_computation | custom fusion | bytes 2304 | tf_op jit(solution)/shard_map/jit(_take)/gather | solution.py:69
  19.4 0.7 all_to_all.32
  20.1 4.9 %all-to-all-start.1 = ((s32[4,1,48]{2,1,0:T(1,128)}), s32[4,1,48]{2,1,0:T(1,128)S(1)}, u32[]{:S(2)}, u32[]{:S(2)}) async-start(s32[4,1,48]{2,1,0:T(1,128)} %all_to_all.32), calls=%async_computation.1 | async-start | bytes 4096 | tf_op jit(solution)/shard_map/all_to_all | solution.py:78
  25.0 0.7 all-gather.5.cloned.1.call-update
  25.7 0.1 broadcast_in_dim.67
  25.9 2.5 %all-gather.7.cloned.1.call-done = bf16[128,4096]{1,0:T(8,128)(2,1)} async-done(((bf16[32,4096]{1,0:T(8,128)(2,1)}), bf16[128,4096]{1,0:T(8,128)(2,1)}) %all-gather.7.cloned.1.call-update) | async-done | bytes 1048592 | tf_op jit(solution)/shard_map/all_gather | solution.py:52
  28.4 1.0 constant_dynamic-slice_fusion
  29.3 1.0 gather_fusion.1
  30.4 0.9 select_select_fusion
  31.2 4.6 %all-to-all-start.2 = ((bf16[4,48,1024]{2,1,0:T(8,128)(2,1)}), bf16[4,48,1024]{2,1,0:T(8,128)(2,1)S(1)}, u32[]{:S(2)}, u32[]{:S(2)}) async-start(bf16[4,48,1024]{2,1,0:T(8,128)(2,1)} %select_select_fusion), calls=%async_computation.2 | async-start | bytes 786432 | tf_op jit(solution)/shard_map/all_to_all | solution.py:71
  35.8 0.5 broadcast.96
  36.3 0.7 reduce.4
  37.1 20.6 %all-to-all-done.2 = bf16[4,48,1024]{2,1,0:T(8,128)(2,1)S(1)} async-done(((bf16[4,48,1024]{2,1,0:T(8,128)(2,1)}), bf16[4,48,1024]{2,1,0:T(8,128)(2,1)S(1)}, u32[]{:S(2)}, u32[]{:S(2)}) %all-to-all-start.2) | async-done | bytes 393248 | tf_op jit(solution)/shard_map/all_to_all | solution.py:71
  57.7 2.3 %fusion.2 = f32[192,64]{0,1:T(8,128)S(1)} fusion(bf16[192,1024,1]{1,0,2:T(8,128)(2,1)S(1)} %bitcast.28, bf16[16,64,1024]{2,1,0:T(8,128)(2,1)} %param.7, f32[192,16]{0,1:T(8,128)S(1)} %get-tuple-element.11), kind=kOutput, calls=%fused_computation.8 | convolution fusion | flops 403034112 | bytes 2551808 | tf_op jit(solution)/shard_map/dot_general | solution.py:18
  60.1 5.8 %all-gather.1 = f32[4,192,64]{1,2,0:T(8,128)S(1)} all-gather(f32[1,192,64]{1,2,0:T(8,128)S(1)} %bitcast.29), channel_id=2, replica_groups=mesh['groups'=2,'pool'=4,'sub'=2,'chip'=2] {'sub','chip'}, dimensions={0}, use_global_device_ids=true | all-gather | bytes 245760 | tf_op jit(solution)/shard_map/all_gather | solution.py:26
  65.9 1.4 %fusion.1 = bf16[192,1024]{1,0:T(8,128)(2,1)} fusion(bf16[16,64,1024]{2,1,0:T(8,128)(2,1)S(1)} %copy-done, bf16[192,64]{0,1:T(8,128)(2,1)S(1)} %reduce_sum.29, bf16[192,16]{0,1:T(8,128)(2,1)S(1)} %get-tuple-element.10), kind=kOutput, calls=%fused_computation.7 | convolution fusion | flops 403243008 | bytes 2521088 | tf_op jit(solution)/shard_map/dot_general | solution.py:33
  67.3 3.5 %all-to-all-start.3 = ((bf16[4,48,1024]{2,1,0:T(8,128)(2,1)}), bf16[4,48,1024]{2,1,0:T(8,128)(2,1)S(1)}, u32[]{:S(2)}, u32[]{:S(2)}) async-start(bf16[4,48,1024]{2,1,0:T(8,128)(2,1)} %bitcast.7), calls=%async_computation.3 | async-start | bytes 786432 | tf_op jit(solution)/shard_map/all_to_all | solution.py:88
  70.7 5.7 %convolution_convert_fusion = bf16[128,1024]{1,0:T(8,128)(2,1)} fusion(bf16[128,4096]{1,0:T(8,128)(2,1)} %all-gather.5.cloned.1.call-done, bf16[4096,1024]{1,0:T(8,128)(2,1)} %param.6), kind=kOutput, calls=%fused_computation.9 | convolution fusion | flops 1073872896 | bytes 9699328 | tf_op jit(solution)/shard_map/dot_general | solution.py:46
  76.4 6.7 %all-to-all-done.3 = bf16[4,48,1024]{2,1,0:T(8,128)(2,1)S(1)} async-done(((bf16[4,48,1024]{2,1,0:T(8,128)(2,1)}), bf16[4,48,1024]{2,1,0:T(8,128)(2,1)S(1)}, u32[]{:S(2)}, u32[]{:S(2)}) %all-to-all-start.3) | async-done | bytes 393248 | tf_op jit(solution)/shard_map/all_to_all | solution.py:88
  83.2 3.4 %all-to-all-start = ((bf16[4,32,1024]{2,1,0:T(8,128)(2,1)}), bf16[4,32,1024]{2,1,0:T(8,128)(2,1)S(1)}, u32[]{:S(2)}, u32[]{:S(2)}) async-start(bf16[4,32,1024]{2,1,0:T(8,128)(2,1)} %bitcast), calls=%async_computation | async-start | bytes 524288 | tf_op jit(solution)/shard_map/all_to_all | solution.py:99
  86.7 0.9 gather_fusion.2
  87.5 0.1 broadcast_select_fusion
  87.6 7.8 %all-to-all-done = bf16[4,32,1024]{2,1,0:T(8,128)(2,1)S(1)} async-done(((bf16[4,32,1024]{2,1,0:T(8,128)(2,1)}), bf16[4,32,1024]{2,1,0:T(8,128)(2,1)S(1)}, u32[]{:S(2)}, u32[]{:S(2)}) %all-to-all-start) | async-done | bytes 262176 | tf_op jit(solution)/shard_map/all_to_all | solution.py:99
  95.4 8.4 %all_to_all.42 = bf16[4,32,1024]{2,1,0:T(8,128)(2,1)S(1)} all-to-all(bf16[4,32,1024]{2,1,0:T(8,128)(2,1)S(1)} %broadcast_select_fusion), channel_id=1, replica_groups=mesh['groups'=2,'pool'=4,'sub'=2,'chip'=2] {'sub','chip'}, dimensions={0} | all-to-all | bytes 524288 | tf_op jit(solution)/shard_map/all_to_all | solution.py:96
  103.9 0.7 copy.9
  (21 shorter events, 0.5 us)
Async XLA Ops:
  6.5 59.4 %copy-start = (bf16[16,64,1024]{2,1,0:T(8,128)(2,1)S(1)}, bf16[16,64,1024]{2,1,0:T(8,128)(2,1)}, u32[]{:S(2)}) copy-start(bf16[16,64,1024]{2,1,0:T(8,128)(2,1)} %param.8) | copy-start | bytes 6291460
  6.5 21.8 %all-gather.7.cloned.1.call-start = ((), (), s32[]{:S(2)}) async-start(), calls=%async_computation.6 | async-start | bytes 1310720 | tf_op jit(solution)/shard_map/all_gather | solution.py:52
  20.1 11.1 %all-to-all-start.1 = ((s32[4,1,48]{2,1,0:T(1,128)}), s32[4,1,48]{2,1,0:T(1,128)S(1)}, u32[]{:S(2)}, u32[]{:S(2)}) async-start(s32[4,1,48]{2,1,0:T(1,128)} %all_to_all.32), calls=%async_computation.1 | async-start | bytes 4096 | tf_op jit(solution)/shard_map/all_to_all | solution.py:78
  25.0 45.8 %all-gather.5.cloned.1.call-start = ((), (), s32[]{:S(2)}) async-start(), calls=%async_computation.5 | async-start | bytes 1310720 | tf_op jit(solution)/shard_map/all_gather | solution.py:47
  31.2 26.5 %all-to-all-start.2 = ((bf16[4,48,1024]{2,1,0:T(8,128)(2,1)}), bf16[4,48,1024]{2,1,0:T(8,128)(2,1)S(1)}, u32[]{:S(2)}, u32[]{:S(2)}) async-start(bf16[4,48,1024]{2,1,0:T(8,128)(2,1)} %select_select_fusion), calls=%async_computation.2 | async-start | bytes 786432 | tf_op jit(solution)/shard_map/all_to_all | solution.py:71
  67.3 15.9 %all-to-all-start.3 = ((bf16[4,48,1024]{2,1,0:T(8,128)(2,1)}), bf16[4,48,1024]{2,1,0:T(8,128)(2,1)S(1)}, u32[]{:S(2)}, u32[]{:S(2)}) async-start(bf16[4,48,1024]{2,1,0:T(8,128)(2,1)} %bitcast.7), calls=%async_computation.3 | async-start | bytes 786432 | tf_op jit(solution)/shard_map/all_to_all | solution.py:88
  83.2 12.3 %all-to-all-start = ((bf16[4,32,1024]{2,1,0:T(8,128)(2,1)}), bf16[4,32,1024]{2,1,0:T(8,128)(2,1)S(1)}, u32[]{:S(2)}, u32[]{:S(2)}) async-start(bf16[4,32,1024]{2,1,0:T(8,128)(2,1)} %bitcast), calls=%async_computation | async-start | bytes 524288 | tf_op jit(solution)/shard_map/all_to_all | solution.py:99
Sparse Core Ops, SparseCore 0:
  8.9 19.4 all-gather.6
  29.9 35.1 all-gather.4
